TPU v7x, 256 devices: a whole 4x4x8 slice. The times are simulated.
256 devices in a mesh: tile: 32 (over z, x_hi, core), group: 8 (over y, x_lo).
Axes of the slice: x: 4 (x_hi: 2, x_lo: 2; x = x_hi * 2 + x_lo), y: 4, z: 8, core: 2. Of those that a mesh axis runs over, the one named last changes fastest.
Arguments:
- object_field: float32 [2, 320, 4096], P(None, 'group', 'tile'), may hold values from -6 to 6
- probe_field: float32 [2, 256, 256], replicated, may hold values from -6 to 6
- amplitudes: float32 [256, 256, 256], P(('tile', 'group')), may hold values from 0 to 4
- row_start: int32 [256], P(('tile', 'group')), may hold values from 0 to 64
- column_start: int32 [256], P(('tile', 'group')), may hold values from 0 to 128
- live_slots: int32 [256], P(('tile', 'group')), may hold values 0 or 1
Outputs:
- new_object: float32 [2, 320, 4096], P(None, 'group', 'tile')
- new_probe: float32 [2, 256, 256], replicated
All inputs are finite; a program needn't handle non-finite values. No bound on the sum of `live_slots` on one device may be relied on, other than what follows from the above.
Results may differ from a plain program's by a relative error of at most 0.0001.
Values sent between devices are 32-bit elements; how exact they have to be, the bound alone decides.
No kernel may reach another device: no remote copies, remote signals or barrier semaphores. Data moves between devices by JAX's collectives and lax.ppermute only.
A program may use at most 64 MiB of HBM per device.

v0:
```python
import math
import jax
import jax.numpy as jnp
from jax import lax
from jax.sharding import PartitionSpec as P

WIN = 256
HALO = 128


def padded_2(value, sides, width):
    for axis, dim in sides:
        count, length = (lax.axis_size(axis), value.shape[dim])
        up = [(i, (i + 1) % count) for i in range(count - 1)]
        down = [(j, i) for i, j in up]
        last = lax.slice_in_dim(value, length - width, length, axis=dim)
        initial = lax.slice_in_dim(value, 0, width, axis=dim)
        before = lax.ppermute(last, axis, up)
        after = lax.ppermute(initial, axis, down)
        value = jnp.concatenate([before, value, after], axis=dim)
    return value


def dft_tables(length):
    counter = jnp.arange(length, dtype=jnp.int32)
    product = counter[:, None] * counter[None, :] % length
    angles = 2.0 * math.pi / length * product.astype(jnp.float32)
    factor = 1.0 / math.sqrt(length)
    return (jnp.cos(angles) * factor, jnp.sin(angles) * factor)


def apply_left(matrix, values):
    return jnp.einsum("jk,pkl->pjl", matrix, values, precision=lax.Precision.HIGHEST)


def apply_right(values, matrix):
    return jnp.einsum("pjk,kl->pjl", values, matrix, precision=lax.Precision.HIGHEST)


def transform(real_part, imag_part, cos_table, sin_table, sign):
    left_real = apply_left(cos_table, real_part) - sign * apply_left(sin_table, imag_part)
    left_imag = apply_left(cos_table, imag_part) + sign * apply_left(sin_table, real_part)
    right_real = apply_right(left_real, cos_table) - sign * apply_right(left_imag, sin_table)
    right_imag = apply_right(left_imag, cos_table) + sign * apply_right(left_real, sin_table)
    return (right_real, right_imag)


def window_terms(windows, probe_field, amplitudes, live_slots, cos_table, sin_table):
    sample_real = windows[:, 0]
    sample_imag = windows[:, 1]
    probe_real = probe_field[0]
    probe_imag = probe_field[1]
    exit_real = probe_real * sample_real - probe_imag * sample_imag
    exit_imag = probe_real * sample_imag + probe_imag * sample_real
    far_real, far_imag = transform(exit_real, exit_imag, cos_table, sin_table, -1.0)
    modulus = jnp.maximum(jnp.sqrt(far_real * far_real + far_imag * far_imag), 0.25)
    factor = 1.0 - amplitudes / modulus
    miss_real, miss_imag = transform(
        far_real * factor, far_imag * factor, cos_table, sin_table, 1.0
    )
    weight = live_slots.astype(jnp.float32)[:, None, None]
    miss_real = miss_real * weight
    miss_imag = miss_imag * weight
    grad_real = probe_real * miss_real + probe_imag * miss_imag
    grad_imag = probe_real * miss_imag - probe_imag * miss_real
    probe_light = weight * (probe_real * probe_real + probe_imag * probe_imag)
    terms = jnp.stack([grad_real, grad_imag, probe_light], axis=1)
    probe_grad = jnp.stack(
        [
            jnp.sum(sample_real * miss_real + sample_imag * miss_imag, axis=0),
            jnp.sum(sample_real * miss_imag - sample_imag * miss_real, axis=0),
        ],
        axis=0,
    )
    window_light = jnp.sum(weight * (sample_real * sample_real + sample_imag * sample_imag), axis=0)
    return (terms, probe_grad, window_light)


def add_windows(accum, terms, top_rows, left_edges):
    zero_index = jnp.zeros((), jnp.int32)
    channels = terms.shape[1]

    def place(slot, current):
        corner = (zero_index, top_rows[slot], left_edges[slot])
        piece = lax.dynamic_slice(current, corner, (channels, WIN, WIN))
        return lax.dynamic_update_slice(current, piece + terms[slot], corner)

    return lax.fori_loop(0, terms.shape[0], place, accum)


def cut_windows(padded, top_rows, left_edges):
    zero_index = jnp.zeros((), jnp.int32)

    def single(top_row, left_edge):
        return lax.dynamic_slice(padded, (zero_index, top_row, left_edge), (2, WIN, WIN))

    return jax.vmap(single)(top_rows, left_edges)


def edge_strips(accum):
    return jnp.concatenate([accum[:, :, :HALO], accum[:, :, accum.shape[2] - HALO :]], axis=2)


def add_edges(inner, arrived):
    width = inner.shape[2]
    inner = inner.at[:, :, :HALO].add(arrived[:, :, :HALO])
    return inner.at[:, :, width - HALO :].add(arrived[:, :, arrived.shape[2] - HALO :])


def apply_updates(object_field, probe_field, share, probe_grad, window_light):
    light_max = jnp.max(probe_field[0] * probe_field[0] + probe_field[1] * probe_field[1]) + 1e-06
    new_object = object_field - share[0:2] / (share[2:3] + 0.25 * light_max)
    new_probe = (
        probe_field - probe_grad / (window_light + 0.25 * jnp.mean(window_light) + 1e-05)[None]
    )
    return (new_object, new_probe)


def local(object_field, probe_field, amplitudes, row_start, column_start, live_slots):
    cos_table, sin_table = dft_tables(WIN)
    full_rows = lax.all_gather(object_field, "group", axis=1, tiled=True)
    padded = padded_2(full_rows, (("tile", 2),), HALO)
    windows = cut_windows(padded, row_start, column_start)
    terms, probe_grad, window_light = window_terms(
        windows, probe_field, amplitudes, live_slots, cos_table, sin_table
    )
    accum = jnp.zeros((terms.shape[1], padded.shape[1], padded.shape[2]), jnp.float32)
    accum = add_windows(accum, terms, row_start, column_start)
    arrived = padded_2(edge_strips(accum), (("tile", 2),), HALO)
    summed = add_edges(accum[:, :, HALO : accum.shape[2] - HALO], arrived)
    share = lax.psum_scatter(summed, "group", scatter_dimension=1, tiled=True)
    probe_grad, window_light = lax.psum((probe_grad, window_light), ("tile", "group"))
    object_field, probe_field = apply_updates(
        object_field, probe_field, share, probe_grad, window_light
    )
    return (object_field, probe_field)


def solution(mesh):
    return jax.shard_map(
        local,
        mesh=mesh,
        in_specs=(
            P(None, "group", "tile"),
            P(),
            P(("tile", "group"), None, None),
            P(("tile", "group")),
            P(("tile", "group")),
            P(("tile", "group")),
        ),
        out_specs=(P(None, "group", "tile"), P()),
        check_vma=False,
    )
```

profile of v0, /device:TPU:2, one launch (start us, length us, event | category | flops | bytes accessed | tf_op | source)
XLA Modules:
  0.0 370.7 jit_solution(3378128131235949026)
XLA Ops:
  8.0 0.0 copy-start
  8.0 0.0 all-reduce.3.cloned.1.call-start
  8.1 29.8 %all_gather.3 = f32[2,320,128]{2,1,0:T(8,128)S(1)} all-gather(f32[2,40,128]{2,1,0:T(8,128)} %param.14), channel_id=1, replica_groups=mesh['tile'=32,'group'=8] {'group'}, dimensions={1}, use_global_device_ids=true | all-gather | bytes 368640 | tf_op jit(solution)/shard_map/all_gather | solution.py:121
  37.9 1.3 collective-permute-start.1
  39.2 3.1 collective-permute-start
  44.2 0.0 collective-permute-done.1
  44.2 0.0 collective-permute-done
  44.2 0.4 fusion.12
  44.6 0.0 copy-done
  44.6 0.1 fusion.40
  44.7 1.5 fusion.38
  46.2 1.5 fusion.34
  47.7 1.5 fusion.9
  49.2 1.5 fusion.7
  50.7 1.5 fusion.47
  52.1 0.0 copy-start.6
  52.2 1.5 fusion.48
  53.6 1.5 fusion.4
  55.1 0.0 copy-done.6
  55.1 1.7 bitcast_multiply_fusion.11
  56.9 1.5 fusion.31
  58.4 1.5 fusion.27
  59.8 1.5 fusion.3
  61.3 1.5 fusion.2
  62.8 1.5 fusion.45
  64.3 1.5 fusion.46
  65.8 1.5 fusion
  67.3 0.0 copy-start.1
  67.3 1.7 fusion.1
  69.0 0.0 copy-start.3
  69.0 0.7 fusion.24
  69.7 0.0 copy-done.1
  69.7 0.1 maximum_bitcast_fusion
  69.8 0.0 copy-done.3
  69.8 0.1 broadcast_in_dim.6
  69.9 10.9 %dynamic_update_slice.4 = f32[3,320,384]{2,1,0:T(8,128)S(1)} dynamic-update-slice(f32[3,320,384]{2,1,0:T(8,128)S(1)} %broadcast_in_dim.6, f32[3,256,256]{2,1,0:T(8,128)S(1)} %maximum_bitcast_fusion, s32[]{:T(128)} %constant.112.clone.1, s32[]{:T(128)S(6)} %select_n.60, s32[]{:T(128)S(6)} %select_n.61) | dynamic-update-slice | bytes 1572868 | tf_op jit(solution)/shard_map/while/body/eval_jaxpr/dynamic_update_slice | solution.py:86
  80.8 0.0 copy-start.2
  80.8 0.0 copy-start.4
  80.8 0.9 fusion.132
  81.6 6.6 %collective-permute-start.2 = (f32[3,320,128]{2,1,0:T(8,128)}, f32[3,320,128]{2,1,0:T(8,128)S(1)}, u32[]{:S(2)}, u32[]{:S(2)}) collective-permute-start(f32[3,320,128]{2,1,0:T(8,128)} %get-tuple-element.73), channel_id=1, source_target_pairs={{0,8},{8,16},{16,24},{24,32},{32,40},{40,48},{48,56},{56,64},{64,7... | collective-permute-start | bytes 1474568 | tf_op jit(solution)/shard_map/ppermute | solution.py:18
  88.2 1.3 collective-permute-start.3
  89.5 0.0 copy-done.2
  89.6 0.0 copy-done.4
  89.6 0.8 fusion.18
  90.4 0.8 pad_maximum_fusion
  91.2 0.0 all-reduce.3.cloned.1.call-update
  91.2 0.0 reduce-scatter.2.cloned.1.call-start
  91.3 0.0 collective-permute-done.2
  91.3 4.5 %collective-permute-done.3 = f32[3,320,128]{2,1,0:T(8,128)} collective-permute-done((f32[3,320,128]{2,1,0:T(8,128)S(1)}, f32[3,320,128]{2,1,0:T(8,128)}, u32[]{:S(2)}, u32[]{:S(2)}) %collective-permute-start.3) | collective-permute-done | bytes 491552 | tf_op jit(solution)/shard_map/ppermute | solution.py:19
  95.7 1.9 fusion.13
  97.6 0.0 copy-start.5
  97.6 0.0 reduce-scatter.2.cloned.1.call-update
  98.3 257.6 %all-reduce.3.cloned.1.call-done = (f32[2,256,256]{2,1,0:T(8,128)}, f32[256,256]{1,0:T(8,128)}) async-done(((f32[2,256,256]{2,1,0:T(8,128)}, f32[256,256]{1,0:T(8,128)}), (f32[2,256,256]{2,1,0:T(8,128)}, f32[256,256]{1,0:T(8,128)})) %all-reduce.3.cloned.1.call-update) | async-done | bytes 786448 | tf_op jit(solution)/shard_map/psum | solution.py:132
  355.9 1.6 reduce_sum.8
  358.2 1.0 add_add_fusion
  359.2 1.9 divide_subtract_fusion
  361.1 0.0 reduce-scatter.2.cloned.1.call-done
  361.1 0.7 fusion.51
  361.8 0.0 copy-done.5
  361.9 1.4 fusion.50
Async XLA Ops:
  8.0 36.6 %copy-start = (f32[2,256,256]{2,1,0:T(8,128)S(1)}, f32[2,256,256]{2,1,0:T(8,128)}, u32[]{:S(2)}) copy-start(f32[2,256,256]{2,1,0:T(8,128)} %param.15) | copy-start | bytes 1572868
  8.0 347.9 %all-reduce.3.cloned.1.call-start = ((), (), s32[]{:S(2)}) async-start(), calls=%async_computation.2 | async-start | bytes 1572864 | tf_op jit(solution)/shard_map/psum | solution.py:132
  37.9 6.3 %collective-permute-start.1 = (f32[2,320,128]{2,1,0:T(8,128)S(1)}, f32[2,320,128]{2,1,0:T(8,128)S(1)}, u32[]{:S(2)}, u32[]{:S(2)}) collective-permute-start(f32[2,320,128]{2,1,0:T(8,128)S(1)} %all_gather.3), channel_id=1, source_target_pairs={{8,0},{16,8},{24,16},{32,24},{40,32},{48,40},{56,48},{64,56},{72,6... | collective-permute-start | bytes 983048 | tf_op jit(solution)/shard_map/ppermute | solution.py:19
  39.2 5.0 %collective-permute-start = (f32[2,320,128]{2,1,0:T(8,128)S(1)}, f32[2,320,128]{2,1,0:T(8,128)S(1)}, u32[]{:S(2)}, u32[]{:S(2)}) collective-permute-start(f32[2,320,128]{2,1,0:T(8,128)S(1)} %all_gather.3), channel_id=1, source_target_pairs={{0,8},{8,16},{16,24},{24,32},{32,40},{40,48},{48,56},{56,64},{64,7... | collective-permute-start | bytes 983048 | tf_op jit(solution)/shard_map/ppermute | solution.py:18
  52.1 3.0 copy-start.6
  67.3 2.4 copy-start.1
  69.0 0.8 copy-start.3
  80.8 8.8 %copy-start.2 = (f32[256,256]{1,0:T(8,128)S(1)}, f32[256,256]{1,0:T(8,128)}, u32[]{:S(2)}) copy-start(f32[256,256]{1,0:T(8,128)} %copy-done.1) | copy-start | bytes 786436
  80.8 8.8 %copy-start.4 = (f32[256,256]{1,0:T(8,128)S(1)}, f32[256,256]{1,0:T(8,128)}, u32[]{:S(2)}) copy-start(f32[256,256]{1,0:T(8,128)} %copy-done.3) | copy-start | bytes 786436
  81.6 9.6 %collective-permute-start.2 = (f32[3,320,128]{2,1,0:T(8,128)}, f32[3,320,128]{2,1,0:T(8,128)S(1)}, u32[]{:S(2)}, u32[]{:S(2)}) collective-permute-start(f32[3,320,128]{2,1,0:T(8,128)} %get-tuple-element.73), channel_id=1, source_target_pairs={{0,8},{8,16},{16,24},{24,32},{32,40},{40,48},{48,56},{56,64},{64,7... | collective-permute-start | bytes 1474568 | tf_op jit(solution)/shard_map/ppermute | solution.py:18
  88.2 7.5 %collective-permute-start.3 = (f32[3,320,128]{2,1,0:T(8,128)S(1)}, f32[3,320,128]{2,1,0:T(8,128)}, u32[]{:S(2)}, u32[]{:S(2)}) collective-permute-start(f32[3,320,128]{2,1,0:T(8,128)S(1)} %get-tuple-element.74), channel_id=1, source_target_pairs={{8,0},{16,8},{24,16},{32,24},{40,32},{48,40},{56,48},{64,56},{72,6... | collective-permute-start | bytes 1474568 | tf_op jit(solution)/shard_map/ppermute | solution.py:19
  91.2 269.9 %reduce-scatter.2.cloned.1.call-start = ((), (), s32[]{:S(2)}) async-start(), calls=%async_computation.1 | async-start | bytes 552960 | tf_op jit(solution)/shard_map/reduce_scatter | solution.py:131
  97.6 264.2 %copy-start.5 = (f32[2,40,128]{2,1,0:T(8,128)S(1)}, f32[2,40,128]{2,1,0:T(8,128)}, u32[]{:S(2)}) copy-start(f32[2,40,128]{2,1,0:T(8,128)} %param.14) | copy-start | bytes 122884
Sparse Core Ops, SparseCore 0:
  91.3 264.5 all-reduce.2
Sparse Core Ops, SparseCore 1:
  97.8 51.0 reduce-scatter.1
where the time goes:
time: 371 us
  waiting for transfers between devices  262 us (71%)
  blocking collectives  29.8 us (8%)
  matrix products  24.1 us (6%)
  between operations  19 us (5%)
  starting transfers between devices  12.3 us (3%)
  local copies, waits for them, and re-layouts  11.9 us (3%)
  other arithmetic  11.4 us (3%)
    psum x1, waiting for transfers between devices, local(): lax.psum((probe_grad, window_light), ('tile', 'group'))  258 us
    all_gather x1, blocking collectives, local(): full_rows = lax.all_gather(object_field, 'group', axis=1, tiled=True)  29.8 us
    dot_general x8, matrix products, apply_right(): jnp.einsum('pjk,kl->pjl', values, matrix, precision=lax.Precision.HIGHEST)  12.3 us
    dot_general x8, matrix products, apply_left(): jnp.einsum('jk,pkl->pjl', matrix, values, precision=lax.Precision.HIGHEST)  11.8 us
    dynamic_update_slice x1, local copies, waits for them, and re-layouts, place(): return lax.dynamic_update_slice(current, piece + terms[slot], corner)  10.9 us
    ppermute x2, starting transfers between devices, padded_2(): before = lax.ppermute(last, axis, up)  9.64 us
  transfers between devices with their start and end apart: 6, of which 2 were waited for; matrix products, arithmetic and copies ran while one was open for 2% of the time, Pallas kernels for 0%

commit v1 on v0

--- a/solution.py
+++ b/solution.py
@@ -118,7 +118,8 @@
 
 def local(object_field, probe_field, amplitudes, row_start, column_start, live_slots):
     cos_table, sin_table = dft_tables(WIN)
-    full_rows = lax.all_gather(object_field, "group", axis=1, tiled=True)
+    sent = jnp.stack([object_field] * lax.axis_size("group"))
+    full_rows = jnp.concatenate(lax.all_to_all(sent, "group", 0, 0), axis=1)
     padded = padded_2(full_rows, (("tile", 2),), HALO)
     windows = cut_windows(padded, row_start, column_start)
     terms, probe_grad, window_light = window_terms(

time: 371 us -> 354 us (0.954)
  blocking collectives: 29.8 us -> 12.7 us
    all_gather x1 -> x0, blocking collectives: 29.8 us -> none  [local(): full_rows = lax.all_gather(object_field, 'group', axis=1, tiled=True)]
    all_to_all x0 -> x1, blocking collectives: none -> 12.7 us  [local(): full_rows = jnp.concatenate(lax.all_to_all(sent, 'group', 0, 0), axis=1)]
where the time goes in v1:
time: 354 us
  waiting for transfers between devices  261 us (74%)
  matrix products  24.1 us (7%)
  between operations  19 us (5%)
  local copies, waits for them, and re-layouts  12.7 us (4%)
  blocking collectives  12.7 us (4%)
  starting transfers between devices  12.3 us (3%)
  other arithmetic  11.4 us (3%)
    psum x1, waiting for transfers between devices, local(): lax.psum((probe_grad, window_light), ('tile', 'group'))  257 us
    all_to_all x1, blocking collectives, local(): full_rows = jnp.concatenate(lax.all_to_all(sent, 'group', 0, 0), axis=1)  12.7 us
    dot_general x8, matrix products, apply_right(): jnp.einsum('pjk,kl->pjl', values, matrix, precision=lax.Precision.HIGHEST)  12.3 us
    dot_general x8, matrix products, apply_left(): jnp.einsum('jk,pkl->pjl', matrix, values, precision=lax.Precision.HIGHEST)  11.8 us
    dynamic_update_slice x1, local copies, waits for them, and re-layouts, place(): return lax.dynamic_update_slice(current, piece + terms[slot], corner)  10.9 us
    ppermute x2, starting transfers between devices, padded_2(): before = lax.ppermute(last, axis, up)  9.62 us
  transfers between devices with their start and end apart: 6, of which 2 were waited for; matrix products, arithmetic and copies ran while one was open for 2% of the time, Pallas kernels for 0%

profile of v1, /device:TPU:2, one launch (start us, length us, event | category | flops | bytes accessed | tf_op | source)
XLA Modules:
  0.0 353.7 jit_solution(11822167341686070802)
XLA Ops:
  8.0 0.0 all-reduce.3.cloned.1.call-start
  8.0 0.8 stack.12
  8.8 0.0 copy-start
  8.9 12.7 %all_to_all.5 = f32[8,2,40,128]{3,2,1,0:T(8,128)S(1)} all-to-all(f32[8,2,40,128]{3,2,1,0:T(8,128)S(1)} %stack.12), channel_id=1, replica_groups=mesh['tile'=32,'group'=8] {'group'}, dimensions={0} | all-to-all | bytes 655360 | tf_op jit(solution)/shard_map/all_to_all | solution.py:122
  21.6 1.3 collective-permute-start.1
  22.9 3.1 collective-permute-start
  27.9 0.0 collective-permute-done.1
  27.9 0.0 collective-permute-done
  27.9 0.4 fusion.12
  28.3 0.0 copy-done
  28.3 0.1 fusion.40
  28.4 1.5 fusion.38
  29.9 1.5 fusion.34
  31.4 1.5 fusion.9
  32.9 1.5 fusion.7
  34.4 1.5 fusion.47
  35.8 0.0 copy-start.6
  35.9 1.5 fusion.48
  37.3 1.5 fusion.4
  38.8 0.0 copy-done.6
  38.8 1.7 bitcast_multiply_fusion.11
  40.6 1.5 fusion.31
  42.1 1.5 fusion.27
  43.5 1.5 fusion.3
  45.0 1.5 fusion.2
  46.5 1.5 fusion.45
  48.0 1.5 fusion.46
  49.5 1.5 fusion
  51.0 0.0 copy-start.1
  51.0 1.7 fusion.1
  52.7 0.0 copy-start.3
  52.7 0.7 fusion.24
  53.4 0.0 copy-done.1
  53.4 0.1 maximum_bitcast_fusion
  53.5 0.0 copy-done.3
  53.5 0.1 broadcast_in_dim.6
  53.6 10.9 %dynamic_update_slice.4 = f32[3,320,384]{2,1,0:T(8,128)S(1)} dynamic-update-slice(f32[3,320,384]{2,1,0:T(8,128)S(1)} %broadcast_in_dim.6, f32[3,256,256]{2,1,0:T(8,128)S(1)} %maximum_bitcast_fusion, s32[]{:T(128)} %constant.112.clone.1, s32[]{:T(128)S(6)} %select_n.60, s32[]{:T(128)S(6)} %select_n.61) | dynamic-update-slice | bytes 1572868 | tf_op jit(solution)/shard_map/while/body/eval_jaxpr/dynamic_update_slice | solution.py:86
  64.5 0.0 copy-start.2
  64.5 0.0 copy-start.4
  64.5 0.9 fusion.132
  65.4 6.6 %collective-permute-start.2 = (f32[3,320,128]{2,1,0:T(8,128)}, f32[3,320,128]{2,1,0:T(8,128)S(1)}, u32[]{:S(2)}, u32[]{:S(2)}) collective-permute-start(f32[3,320,128]{2,1,0:T(8,128)} %get-tuple-element.73), channel_id=1, source_target_pairs={{0,8},{8,16},{16,24},{24,32},{32,40},{40,48},{48,56},{56,64},{64,7... | collective-permute-start | bytes 1474568 | tf_op jit(solution)/shard_map/ppermute | solution.py:18
  71.9 1.3 collective-permute-start.3
  73.2 0.0 copy-done.2
  73.2 0.0 copy-done.4
  73.2 0.8 fusion.18
  74.0 0.8 pad_maximum_fusion
  74.9 0.0 all-reduce.3.cloned.1.call-update
  74.9 0.0 reduce-scatter.2.cloned.1.call-start
  74.9 0.0 collective-permute-done.2
  74.9 4.5 %collective-permute-done.3 = f32[3,320,128]{2,1,0:T(8,128)} collective-permute-done((f32[3,320,128]{2,1,0:T(8,128)S(1)}, f32[3,320,128]{2,1,0:T(8,128)}, u32[]{:S(2)}, u32[]{:S(2)}) %collective-permute-start.3) | collective-permute-done | bytes 491552 | tf_op jit(solution)/shard_map/ppermute | solution.py:19
  79.4 1.9 fusion.13
  81.3 0.0 copy-start.5
  81.3 0.0 reduce-scatter.2.cloned.1.call-update
  82.0 256.9 %all-reduce.3.cloned.1.call-done = (f32[2,256,256]{2,1,0:T(8,128)}, f32[256,256]{1,0:T(8,128)}) async-done(((f32[2,256,256]{2,1,0:T(8,128)}, f32[256,256]{1,0:T(8,128)}), (f32[2,256,256]{2,1,0:T(8,128)}, f32[256,256]{1,0:T(8,128)})) %all-reduce.3.cloned.1.call-update) | async-done | bytes 786448 | tf_op jit(solution)/shard_map/psum | solution.py:133
  338.9 1.6 reduce_sum.8
  341.2 1.0 add_add_fusion
  342.2 1.9 divide_subtract_fusion
  344.1 0.0 reduce-scatter.2.cloned.1.call-done
  344.1 0.7 fusion.51
  344.8 0.0 copy-done.5
  344.8 1.4 fusion.50
  (1 shorter events, 0.0 us)
Async XLA Ops:
  8.0 330.9 %all-reduce.3.cloned.1.call-start = ((), (), s32[]{:S(2)}) async-start(), calls=%async_computation.3 | async-start | bytes 1572864 | tf_op jit(solution)/shard_map/psum | solution.py:133
  8.8 19.5 %copy-start = (f32[2,256,256]{2,1,0:T(8,128)S(1)}, f32[2,256,256]{2,1,0:T(8,128)}, u32[]{:S(2)}) copy-start(f32[2,256,256]{2,1,0:T(8,128)} %param.15) | copy-start | bytes 1572868
  21.6 6.3 %collective-permute-start.1 = (f32[2,320,128]{2,1,0:T(8,128)S(1)}, f32[2,320,128]{2,1,0:T(8,128)S(1)}, u32[]{:S(2)}, u32[]{:S(2)}) collective-permute-start(f32[2,320,128]{2,1,0:T(8,128)S(1)} %bitcast.152), channel_id=1, source_target_pairs={{8,0},{16,8},{24,16},{32,24},{40,32},{48,40},{56,48},{64,56},{72,6... | collective-permute-start | bytes 983048 | tf_op jit(solution)/shard_map/ppermute | solution.py:19
  22.9 5.0 %collective-permute-start = (f32[2,320,128]{2,1,0:T(8,128)S(1)}, f32[2,320,128]{2,1,0:T(8,128)S(1)}, u32[]{:S(2)}, u32[]{:S(2)}) collective-permute-start(f32[2,320,128]{2,1,0:T(8,128)S(1)} %bitcast.153), channel_id=1, source_target_pairs={{0,8},{8,16},{16,24},{24,32},{32,40},{40,48},{48,56},{56,64},{64,7... | collective-permute-start | bytes 983048 | tf_op jit(solution)/shard_map/ppermute | solution.py:18
  35.8 3.0 copy-start.6
  51.0 2.4 copy-start.1
  52.7 0.8 copy-start.3
  64.5 8.8 %copy-start.2 = (f32[256,256]{1,0:T(8,128)S(1)}, f32[256,256]{1,0:T(8,128)}, u32[]{:S(2)}) copy-start(f32[256,256]{1,0:T(8,128)} %copy-done.1) | copy-start | bytes 786436
  64.5 8.8 %copy-start.4 = (f32[256,256]{1,0:T(8,128)S(1)}, f32[256,256]{1,0:T(8,128)}, u32[]{:S(2)}) copy-start(f32[256,256]{1,0:T(8,128)} %copy-done.3) | copy-start | bytes 786436
  65.4 9.6 %collective-permute-start.2 = (f32[3,320,128]{2,1,0:T(8,128)}, f32[3,320,128]{2,1,0:T(8,128)S(1)}, u32[]{:S(2)}, u32[]{:S(2)}) collective-permute-start(f32[3,320,128]{2,1,0:T(8,128)} %get-tuple-element.73), channel_id=1, source_target_pairs={{0,8},{8,16},{16,24},{24,32},{32,40},{40,48},{48,56},{56,64},{64,7... | collective-permute-start | bytes 1474568 | tf_op jit(solution)/shard_map/ppermute | solution.py:18
  71.9 7.5 %collective-permute-start.3 = (f32[3,320,128]{2,1,0:T(8,128)S(1)}, f32[3,320,128]{2,1,0:T(8,128)}, u32[]{:S(2)}, u32[]{:S(2)}) collective-permute-start(f32[3,320,128]{2,1,0:T(8,128)S(1)} %get-tuple-element.74), channel_id=1, source_target_pairs={{8,0},{16,8},{24,16},{32,24},{40,32},{48,40},{56,48},{64,56},{72,6... | collective-permute-start | bytes 1474568 | tf_op jit(solution)/shard_map/ppermute | solution.py:19
  74.9 269.2 %reduce-scatter.2.cloned.1.call-start = ((), (), s32[]{:S(2)}) async-start(), calls=%async_computation.2 | async-start | bytes 552960 | tf_op jit(solution)/shard_map/reduce_scatter | solution.py:132
  81.3 263.5 %copy-start.5 = (f32[2,40,128]{2,1,0:T(8,128)S(1)}, f32[2,40,128]{2,1,0:T(8,128)}, u32[]{:S(2)}) copy-start(f32[2,40,128]{2,1,0:T(8,128)} %param.14) | copy-start | bytes 122884
Sparse Core Ops, SparseCore 0:
  75.0 263.8 all-reduce.2
Sparse Core Ops, SparseCore 1:
  81.4 50.2 reduce-scatter.1
